TPU v7x, 32 devices: a whole 2x2x4 slice. The times are simulated.
32 devices in a mesh: grp: 2 (over y), tile: 4 (over z), span: 4 (over x, core).
Axes of the slice: x: 2, y: 2, z: 4, core: 2. Of those that a mesh axis runs over, the one named last changes fastest.
Arguments:
- features: bfloat16 [16, 8, 160, 384], P(('grp', 'span'), 'tile'), parts along dimension 0, may hold values from -24 to 24
- clip_lengths: int32 [8], P('grp'), parts along dimension 0, may hold values from 1 to 4, as said below
- norm_gain: float32 [384], replicated, may hold values from 0.1 to 1.9
- w_qkv: bfloat16 [384, 1152], replicated, may hold values from -6 to 6
- w_out: bfloat16 [384, 384], replicated, may hold values from -1 to 1
- conv_gain: float32 [384], replicated, may hold values from 0.1 to 1.9
- w_conv: bfloat16 [3, 3, 3, 384, 384], replicated, may hold values from -0.0625 to 0.0625
Outputs:
- attended: bfloat16 [16, 8, 160, 384], P(('grp', 'span'), 'tile'), parts along dimension 0
- hidden: bfloat16 [16, 8, 160, 384], P(('grp', 'span'), 'tile'), parts along dimension 0
There are 2 independent parts, one for each index of `grp`. A program takes and returns all parts, laid end to end along the dimension named above; an argument that names none is the same for every part. Nothing has to cross between parts.
Inputs may be any that keep to these rules, and one draw needn't show every extreme that they name: `clip_lengths`: the lengths sum to 8; exactly one clip has 4 frames.
All inputs are finite; a program needn't handle non-finite values.
Results may differ from a plain program's by a relative error of at most 0.0095.
The roundings to bfloat16 on the way count: a program that leaves them out, or rounds other values in their place, can miss the bound.
Values may be sent and summed in bfloat16 or wider, within the bound.
No kernel may reach another device: no remote copies, remote signals or barrier semaphores. Data moves between devices by JAX's collectives and lax.ppermute only.
A program may use at most 128 MiB of HBM per device.

v0:
```python
import jax
import jax.numpy as jnp
from jax import lax
from jax.sharding import PartitionSpec as P

eps = 1e-06


def from_behind(block, axis, distance):
    devices = range(lax.axis_size(axis))
    route = [(i - distance, i) for i in devices if i - distance in devices]
    return lax.ppermute(block, axis, route)


def extended(x, sides, width):
    for axis, dim in sides:
        size, length = (lax.axis_size(axis), x.shape[dim])
        up = [(i, (i + 1) % size) for i in range(size - 1)]
        down = [(j, i) for i, j in up]
        last = lax.slice_in_dim(x, length - width, length, axis=dim)
        first = lax.slice_in_dim(x, 0, width, axis=dim)
        before = lax.ppermute(last, axis, up)
        after = lax.ppermute(first, axis, down)
        x = jnp.concatenate([before, x, after], axis=dim)
    return x


def rms_scale(values, gain_vec):
    as_float = values.astype(jnp.float32)
    return (
        as_float * lax.rsqrt(jnp.mean(as_float * as_float, axis=-1, keepdims=True) + eps) * gain_vec
    )


def on_device(features, clip_lengths, norm_gain, w_qkv, w_out, conv_gain, w_conv):
    frames, row_count, col_count, channels = features.shape
    cell_count = row_count * col_count
    normed_grid = rms_scale(features, norm_gain).astype(jnp.bfloat16)
    view_frames = normed_grid.shape[0]
    view_cells = normed_grid.shape[1] * normed_grid.shape[2]
    normed = normed_grid.reshape(view_frames, view_cells, channels)
    queries = jnp.dot(
        normed.reshape(-1, channels), w_qkv[:, :channels], preferred_element_type=jnp.float32
    )
    queries = queries.astype(jnp.bfloat16).reshape(view_frames, view_cells, channels)
    kv_weight = w_qkv[:, channels:]
    score_scale = channels ** (-0.5)
    outgoing = jnp.dot(normed.reshape(-1, channels), kv_weight, preferred_element_type=jnp.float32)
    outgoing = outgoing.astype(jnp.bfloat16).reshape(view_frames, view_cells, 2 * channels)
    portion = lax.all_gather(outgoing, "tile", axis=1, tiled=True)
    key_part = portion[:, :, :channels]
    value_part = portion[:, :, channels:]
    row_top = jnp.full((view_frames, view_cells, 1), -1e30, jnp.float32)
    scores = (
        jnp.einsum("fqc,fkc->fqk", queries, key_part, preferred_element_type=jnp.float32)
        * score_scale
    )
    new_top = jnp.maximum(row_top, jnp.max(scores, axis=2, keepdims=True))
    raised_f = jnp.exp(scores - new_top)
    row_total = jnp.sum(raised_f, axis=2, keepdims=True)
    weighted = jnp.einsum(
        "fqk,fkc->fqc",
        raised_f.astype(jnp.bfloat16),
        value_part,
        preferred_element_type=jnp.float32,
    )
    mixture_grid = (weighted / row_total).astype(jnp.bfloat16)
    mixture = mixture_grid.reshape(-1, channels)
    projected = jnp.dot(mixture, w_out, preferred_element_type=jnp.float32)
    attended = (features.reshape(-1, channels).astype(jnp.float32) + projected).astype(jnp.bfloat16)
    attended = attended.reshape(frames, row_count, col_count, channels)
    lifted = rms_scale(attended, conv_gain)
    activated = (lifted * jax.nn.sigmoid(lifted)).astype(jnp.bfloat16)
    earlier = from_behind(activated, "span", 1)
    stacked = jnp.concatenate([earlier, activated], axis=0)
    edged = extended(stacked, (("tile", 1),), 1)
    padded = jnp.pad(edged, ((0, 0), (0, 0), (1, 1), (0, 0)))
    clip_ends = jnp.cumsum(clip_lengths)
    position = lax.axis_index("span") * frames + jnp.arange(frames, dtype=jnp.int32)
    clip_start = jnp.sum(
        jnp.where(clip_ends[None, :] <= position[:, None], clip_lengths[None, :], 0), axis=1
    )
    summed = jnp.zeros((frames * cell_count, channels), jnp.float32)
    for t_tap in range(3):
        usable = position - (2 - t_tap) >= clip_start
        for r_tap in range(3):
            for c_tap in range(3):
                shifted = padded[
                    t_tap : t_tap + frames, r_tap : r_tap + row_count, c_tap : c_tap + col_count
                ]
                shifted = jnp.where(
                    usable[:, None, None, None], shifted, jnp.zeros((), shifted.dtype)
                )
                summed = summed + jnp.dot(
                    shifted.reshape(-1, channels),
                    w_conv[t_tap, r_tap, c_tap],
                    preferred_element_type=jnp.float32,
                )
    hidden = summed.astype(jnp.bfloat16).reshape(frames, row_count, col_count, channels)
    return (attended, hidden)


def solution(mesh):
    in_specs = (P(("grp", "span"), "tile", None, None), P("grp"), P(), P(), P(), P(), P())
    out_specs = (P(("grp", "span"), "tile", None, None), P(("grp", "span"), "tile", None, None))
    return jax.shard_map(
        on_device, mesh=mesh, in_specs=in_specs, out_specs=out_specs, check_vma=False
    )
```

profile of v0, /device:TPU:10, one launch (start us, length us, event | category | flops | bytes accessed | tf_op | source)
XLA Modules:
  0.0 146.0 jit_solution(7980055820085720016)
XLA Ops:
  7.2 1.3 multiply_reduce_fusion
  8.5 1.2 multiply_convert_fusion.1
  9.8 2.7 %convolution_convert_fusion = bf16[640,768]{1,0:T(8,128)(2,1)} fusion(bf16[640,384]{1,0:T(8,128)(2,1)S(1)} %bitcast.177, bf16[384,1152]{1,0:T(8,128)(2,1)} %param.10), kind=kOutput, calls=%fused_computation.18 | convolution fusion | flops 377978880 | bytes 2064384 | tf_op jit(solution)/shard_map/dot_general | solution.py:48
  12.5 1.4 convolution_convert_fusion.1
  13.9 73.9 %all-gather.2.cloned.1.call-done = bf16[2,1280,768]{2,1,0:T(8,128)(2,1)} async-done(((bf16[2,320,768]{2,1,0:T(8,128)(2,1)}), bf16[2,1280,768]{2,1,0:T(8,128)(2,1)}) %all-gather.2.cloned.1.call-update) | async-done | bytes 3932176 | tf_op jit(solution)/shard_map/all_gather | solution.py:50
  87.8 2.8 %fusion.98 = (f32[2,320]{1,0:T(2,128)S(1)}, f32[2,320,1280]{2,1,0:T(8,128)S(1)}) fusion(bf16[2,320,384]{2,1,0:T(8,128)(2,1)S(1)} %bitcast.179, bf16[2,1280,768]{2,1,0:T(8,128)(2,1)} %all-gather.2.cloned.1.call-done), kind=kOutput, calls=%fused_computation.171 | convolution fusion | flops 630783360 | bytes 5736960 | tf_op jit(solution)/shard_map/fqc,fkc->fqk/dot_general | solution.py:55
  90.6 0.6 fusion.1
  91.3 1.1 divide_convert_fusion
  92.4 0.6 fusion.14
  93.1 0.4 multiply_convert_fusion
  93.5 1.9 %collective-permute-start = (bf16[2,2,160,384]{3,2,1,0:T(8,128)(2,1)S(1)}, bf16[2,2,160,384]{3,2,1,0:T(8,128)(2,1)S(1)}, u32[]{:S(2)}, u32[]{:S(2)}) collective-permute-start(bf16[2,2,160,384]{3,2,1,0:T(8,128)(2,1)S(1)} %multiply_convert_fusion), channel_id=1, source_target_pairs={{0,1},{1,2},{2,3},{4,5},{5,6},{6,7},{8,9},{9,10},{10,11},{12,13},{... | collective-permute-start | bytes 1474568 | tf_op jit(solution)/shard_map/ppermute | solution.py:12
  95.4 8.2 %collective-permute-done = bf16[2,2,160,384]{3,2,1,0:T(8,128)(2,1)S(1)} collective-permute-done((bf16[2,2,160,384]{3,2,1,0:T(8,128)(2,1)S(1)}, bf16[2,2,160,384]{3,2,1,0:T(8,128)(2,1)S(1)}, u32[]{:S(2)}, u32[]{:S(2)}) %collective-permute-start) | collective-permute-done | bytes 491552 | tf_op jit(solution)/shard_map/ppermute | solution.py:12
  103.6 0.9 fusion.30
  104.5 4.4 %collective-permute-start.1 = (bf16[4,1,160,384]{3,2,1,0:T(8,128)(2,1)}, bf16[4,1,160,384]{3,2,1,0:T(8,128)(2,1)S(1)}, u32[]{:S(2)}, u32[]{:S(2)}) collective-permute-start(bf16[4,1,160,384]{3,2,1,0:T(8,128)(2,1)} %get-tuple-element.34), channel_id=1, source_target_pairs={{0,4},{4,8},{8,12},{1,5},{5,9},{9,13},{2,6},{6,10},{10,14},{3,7},{... | collective-permute-start | bytes 1474568 | tf_op jit(solution)/shard_map/ppermute | solution.py:22
  108.9 1.9 %collective-permute-start.2 = (bf16[4,1,160,384]{3,2,1,0:T(8,128)(2,1)S(1)}, bf16[4,1,160,384]{3,2,1,0:T(8,128)(2,1)S(1)}, u32[]{:S(2)}, u32[]{:S(2)}) collective-permute-start(bf16[4,1,160,384]{3,2,1,0:T(8,128)(2,1)S(1)} %get-tuple-element.35), channel_id=1, source_target_pairs={{4,0},{8,4},{12,8},{5,1},{9,5},{13,9},{6,2},{10,6},{14,10},{7,3},{... | collective-permute-start | bytes 1474568 | tf_op jit(solution)/shard_map/ppermute | solution.py:23
  111.4 4.4 %collective-permute-done.1 = bf16[4,1,160,384]{3,2,1,0:T(8,128)(2,1)S(1)} collective-permute-done((bf16[4,1,160,384]{3,2,1,0:T(8,128)(2,1)}, bf16[4,1,160,384]{3,2,1,0:T(8,128)(2,1)S(1)}, u32[]{:S(2)}, u32[]{:S(2)}) %collective-permute-start.1) | collective-permute-done | bytes 491552 | tf_op jit(solution)/shard_map/ppermute | solution.py:22
  115.8 3.9 %collective-permute-done.2 = bf16[4,1,160,384]{3,2,1,0:T(8,128)(2,1)S(1)} collective-permute-done((bf16[4,1,160,384]{3,2,1,0:T(8,128)(2,1)S(1)}, bf16[4,1,160,384]{3,2,1,0:T(8,128)(2,1)S(1)}, u32[]{:S(2)}, u32[]{:S(2)}) %collective-permute-start.2) | collective-permute-done | bytes 491552 | tf_op jit(solution)/shard_map/ppermute | solution.py:23
  119.6 1.2 select_maximum_fusion
  120.8 1.4 slice_select_fusion
  122.5 1.5 %slice_select_fusion.6 = (bf16[2,2,160,384]{3,2,1,0:T(8,128)(2,1)S(1)}, bf16[2,2,160,384]{3,2,1,0:T(8,128)(2,1)S(1)}, bf16[2,2,160,384]{3,2,1,0:T(8,128)(2,1)S(1...) fusion(bf16[4,3,160,384]{3,2,1,0:T(8,128)(2,1)S(1)} %get-tuple-, ...), kind=kLoop, calls=%fused_computation.77 | loop fusion | flops 3686400 | bytes 13762566 | tf_op jit(solution)/shard_map/jit(_where)/select_n | solution.py:91
  124.3 1.3 slice-done.1
  125.6 0.4 fusion.62
  126.1 0.4 fusion.57
  126.5 0.5 convolution_add_fusion.24
  127.0 0.5 convolution_add_fusion.23
  127.5 0.5 convolution_add_fusion.22
  128.0 0.5 fusion.11
  128.4 0.5 convolution_add_fusion.20
  128.9 0.5 convolution_add_fusion.19
  129.4 0.5 convolution_add_fusion.18
  129.8 0.5 convolution_add_fusion.17
  130.3 0.5 convolution_add_fusion.16
  130.8 0.5 convolution_add_fusion.15
  131.2 0.5 convolution_add_fusion.14
  131.7 0.5 convolution_add_fusion.13
  132.1 0.5 convolution_add_fusion.12
  132.6 0.5 convolution_add_fusion.11
  133.1 0.5 convolution_add_fusion.10
  133.5 0.5 convolution_add_fusion.9
  134.0 0.5 convolution_add_fusion.8
  134.4 0.4 convolution_add_fusion.7
  134.9 0.5 convolution_add_fusion.6
  135.4 0.5 convolution_add_fusion.5
  135.8 0.6 convolution_add_fusion.4
  136.5 0.5 convolution_add_fusion.3
  137.0 0.5 convolution_add_fusion.2
  137.4 0.4 convolution_add_fusion.1
  137.9 1.2 fusion.13
  (29 shorter events, 1.2 us)
Async XLA Ops:
  7.2 85.3 %copy-start = (bf16[384,384]{1,0:T(8,128)(2,1)S(1)}, bf16[384,384]{1,0:T(8,128)(2,1)}, u32[]{:S(2)}) copy-start(bf16[384,384]{1,0:T(8,128)(2,1)} %param.11) | copy-start | bytes 884740
  7.2 80.6 %all-gather.2.cloned.1.call-start = ((), (), s32[]{:S(2)}) async-start(), calls=%async_computation | async-start | bytes 4915200 | tf_op jit(solution)/shard_map/all_gather | solution.py:50
  87.8 3.5 %copy-start.2 = (bf16[2,1280,768]{2,1,0:T(8,128)(2,1)S(1)}, bf16[2,1280,768]{2,1,0:T(8,128)(2,1)}, u32[]{:S(2)}) copy-start(bf16[2,1280,768]{2,1,0:T(8,128)(2,1)} %all-gather.2.cloned.1.call-done) | copy-start | bytes 11796484
  91.3 1.1 copy-start.1
  91.3 1.8 %copy-start.4 = (f32[384]{0:T(512)S(1)}, f32[384]{0:T(512)}, u32[]{:S(2)}) copy-start(f32[384]{0:T(512)} %param.12) | copy-start | bytes 4612
  92.4 18.4 %copy-start.5 = (s32[4]{0:T(128)S(1)}, s32[4]{0:T(128)}, u32[]{:S(2)}) copy-start(s32[4]{0:T(128)} %param.8) | copy-start | bytes 52
  93.0 42.8 %copy-start.3 = (bf16[640,384]{1,0:T(8,128)(2,1)}, bf16[640,384]{1,0:T(8,128)(2,1)S(1)}, u32[]{:S(2)}) copy-start(bf16[640,384]{1,0:T(8,128)(2,1)S(1)} %get-tuple-element.55) | copy-start | bytes 1474564
  93.5 10.1 %collective-permute-start = (bf16[2,2,160,384]{3,2,1,0:T(8,128)(2,1)S(1)}, bf16[2,2,160,384]{3,2,1,0:T(8,128)(2,1)S(1)}, u32[]{:S(2)}, u32[]{:S(2)}) collective-permute-start(bf16[2,2,160,384]{3,2,1,0:T(8,128)(2,1)S(1)} %multiply_convert_fusion), channel_id=1, source_target_pairs={{0,1},{1,2},{2,3},{4,5},{5,6},{6,7},{8,9},{9,10},{10,11},{12,13},{... | collective-permute-start | bytes 1474568 | tf_op jit(solution)/shard_map/ppermute | solution.py:12
  104.5 11.2 %collective-permute-start.1 = (bf16[4,1,160,384]{3,2,1,0:T(8,128)(2,1)}, bf16[4,1,160,384]{3,2,1,0:T(8,128)(2,1)S(1)}, u32[]{:S(2)}, u32[]{:S(2)}) collective-permute-start(bf16[4,1,160,384]{3,2,1,0:T(8,128)(2,1)} %get-tuple-element.34), channel_id=1, source_target_pairs={{0,4},{4,8},{8,12},{1,5},{5,9},{9,13},{2,6},{6,10},{10,14},{3,7},{... | collective-permute-start | bytes 1474568 | tf_op jit(solution)/shard_map/ppermute | solution.py:22
  108.9 10.7 %collective-permute-start.2 = (bf16[4,1,160,384]{3,2,1,0:T(8,128)(2,1)S(1)}, bf16[4,1,160,384]{3,2,1,0:T(8,128)(2,1)S(1)}, u32[]{:S(2)}, u32[]{:S(2)}) collective-permute-start(bf16[4,1,160,384]{3,2,1,0:T(8,128)(2,1)S(1)} %get-tuple-element.35), channel_id=1, source_target_pairs={{4,0},{8,4},{12,8},{5,1},{9,5},{13,9},{6,2},{10,6},{14,10},{7,3},{... | collective-permute-start | bytes 1474568 | tf_op jit(solution)/shard_map/ppermute | solution.py:23
  122.2 2.1 %slice-start = ((s8[7962624]{0:T(1024)(128)(4,1)}), s8[3768320]{0:T(1024)(128)(4,1)S(1)}, s32[]{:S(2)}) async-start(s8[7962624]{0:T(1024)(128)(4,1)} %bitcast.148), calls=%async_computation.1 | async-start | bytes 7536640
  122.5 3.1 %slice-start.1 = ((s8[7962624]{0:T(1024)(128)(4,1)}), s8[4194304]{0:T(1024)(128)(4,1)S(1)}, s32[]{:S(2)}) async-start(s8[7962624]{0:T(1024)(128)(4,1)} %bitcast.148), calls=%async_computation.2 | async-start | bytes 8388608
Sparse Core Ops, SparseCore 0:
  12.6 75.1 all-gather.1
where the time goes:
time: 146 us
  waiting for transfers between devices  90.4 us (62%)
  matrix products  21.9 us (15%)
  between operations  14.4 us (10%)
  other arithmetic  9.18 us (6%)
  starting transfers between devices  8.25 us (6%)
  local copies, waits for them, and re-layouts  1.85 us (1%)
    all_gather x1, waiting for transfers between devices, on_device(): portion = lax.all_gather(outgoing, 'tile', axis=1, tiled=True)  73.9 us
    dot_general x27, matrix products, on_device(): jnp.dot(shifted.reshape(-1, channels), w_conv[t_tap, r_tap, c_tap], prefe...  13.3 us
    ppermute x1, waiting for transfers between devices, from_behind(): return lax.ppermute(block, axis, route)  8.22 us
    ppermute x1, starting transfers between devices, extended(): before = lax.ppermute(last, axis, up)  4.37 us
    ppermute x1, waiting for transfers between devices, extended(): before = lax.ppermute(last, axis, up)  4.36 us
    ppermute x1, waiting for transfers between devices, extended(): after = lax.ppermute(first, axis, down)  3.87 us
    select_n x2, other arithmetic, on_device(): jnp.where(usable[:, None, None, None], shifted, jnp.zeros((), shifted.dty...  2.92 us
  transfers between devices with their start and end apart: 4, of which 4 were waited for; matrix products, arithmetic and copies ran while one was open for 1% of the time, Pallas kernels for 0%

commit v1 on v0

--- a/solution.py
+++ b/solution.py
@@ -47,7 +47,12 @@
     score_scale = channels ** (-0.5)
     outgoing = jnp.dot(normed.reshape(-1, channels), kv_weight, preferred_element_type=jnp.float32)
     outgoing = outgoing.astype(jnp.bfloat16).reshape(view_frames, view_cells, 2 * channels)
-    portion = lax.all_gather(outgoing, "tile", axis=1, tiled=True)
+    ring = [outgoing]
+    for hop in range(3):
+        ring.append(lax.ppermute(ring[-1], "tile", [(dev, (dev + 1) % 4) for dev in range(4)]))
+    portion = jnp.roll(
+        jnp.concatenate(ring[::-1], axis=1), (lax.axis_index("tile") + 1) * ring[0].shape[1], axis=1
+    )
     key_part = portion[:, :, :channels]
     value_part = portion[:, :, channels:]
     row_top = jnp.full((view_frames, view_cells, 1), -1e30, jnp.float32)

time: 146 us -> 130 us (0.89)
  between operations: 14.4 us -> 1.12 us
  waiting for transfers between devices: 90.4 us -> 81.2 us
  starting transfers between devices: 8.25 us -> 13.4 us
  local copies, waits for them, and re-layouts: 1.85 us -> 4.79 us
  matrix products: 21.9 us -> 20.1 us
    all_gather x1 -> x0, waiting for transfers between devices: 73.9 us -> none  [on_device(): portion = lax.all_gather(outgoing, 'tile', axis=1, tiled=True)]
    ppermute x0 -> x3, waiting for transfers between devices: none -> 64.7 us  [on_device(): lax.ppermute(ring[-1], 'tile', [(dev, (dev + 1) % 4) for dev in range(4)])]
    ppermute x0 -> x3, starting transfers between devices: none -> 4.14 us  [on_device(): lax.ppermute(ring[-1], 'tile', [(dev, (dev + 1) % 4) for dev in range(4)])]
    ppermute x1, starting transfers between devices: 1.92 us -> 5.44 us  [extended(): after = lax.ppermute(first, axis, down)]
    unnamed x16 -> x25, local copies, waits for them, and re-layouts: 1.61 us -> 4.48 us
    ppermute x1, starting transfers between devices: 4.37 us -> 1.92 us  [extended(): before = lax.ppermute(last, axis, up)]
    dot_general x1, matrix products: 2.83 us -> 1.18 us  [on_device(): jnp.einsum('fqc,fkc->fqk', queries, key_part, preferred_element_type=jnp....]
  transfers between devices with their start and end apart: 4 -> 6, of which waited for: 4 -> 6; matrix products, arithmetic and copies ran while one was open for 1% -> 2% of each run, Pallas kernels for 0% -> 0%
where the time goes in v1:
time: 130 us
  waiting for transfers between devices  81.2 us (62%)
  matrix products  20.1 us (15%)
  starting transfers between devices  13.4 us (10%)
  other arithmetic  9.18 us (7%)
  local copies, waits for them, and re-layouts  4.79 us (4%)
    ppermute x3, waiting for transfers between devices, on_device(): lax.ppermute(ring[-1], 'tile', [(dev, (dev + 1) % 4) for dev in range(4)])  64.7 us
    dot_general x27, matrix products, on_device(): jnp.dot(shifted.reshape(-1, channels), w_conv[t_tap, r_tap, c_tap], prefe...  13.3 us
    ppermute x1, waiting for transfers between devices, from_behind(): return lax.ppermute(block, axis, route)  8.22 us
    ppermute x1, starting transfers between devices, extended(): after = lax.ppermute(first, axis, down)  5.44 us
    unnamed x25, local copies, waits for them, and re-layouts  4.48 us
    ppermute x1, waiting for transfers between devices, extended(): after = lax.ppermute(first, axis, down)  4.16 us
    ppermute x3, starting transfers between devices, on_device(): lax.ppermute(ring[-1], 'tile', [(dev, (dev + 1) % 4) for dev in range(4)])  4.14 us
    ppermute x1, waiting for transfers between devices, extended(): before = lax.ppermute(last, axis, up)  4.08 us
  transfers between devices with their start and end apart: 6, of which 6 were waited for; matrix products, arithmetic and copies ran while one was open for 2% of the time, Pallas kernels for 0%

profile of v1, /device:TPU:10, one launch (start us, length us, event | category | flops | bytes accessed | tf_op | source)
XLA Modules:
  0.0 129.8 jit_solution(6268828413121387253)
XLA Ops:
  0.6 1.3 multiply_reduce_fusion
  2.0 1.2 multiply_convert_fusion.1
  3.2 1.9 %convolution_convert_fusion = bf16[640,768]{1,0:T(8,128)(2,1)S(1)} fusion(bf16[640,384]{1,0:T(8,128)(2,1)S(1)} %bitcast.170, bf16[384,1152]{1,0:T(8,128)(2,1)} %param.10), kind=kOutput, calls=%fused_computation.18 | convolution fusion | flops 377978880 | bytes 2064384 | tf_op jit(solution)/shard_map/dot_general | solution.py:48
  5.1 1.6 %collective-permute-start = (bf16[2,320,768]{2,1,0:T(8,128)(2,1)S(1)}, bf16[2,320,768]{2,1,0:T(8,128)(2,1)S(1)}, u32[]{:S(2)}, u32[]{:S(2)}) collective-permute-start(bf16[2,320,768]{2,1,0:T(8,128)(2,1)S(1)} %bitcast.150), channel_id=1, source_target_pairs={{0,4},{4,8},{8,12},{12,0},{1,5},{5,9},{9,13},{13,1},{2,6},{6,10},{... | collective-permute-start | bytes 2949128 | tf_op jit(solution)/shard_map/ppermute | solution.py:52
  6.7 21.9 %collective-permute-done = bf16[2,320,768]{2,1,0:T(8,128)(2,1)S(1)} collective-permute-done((bf16[2,320,768]{2,1,0:T(8,128)(2,1)S(1)}, bf16[2,320,768]{2,1,0:T(8,128)(2,1)S(1)}, u32[]{:S(2)}, u32[]{:S(2)}) %collective-permute-start) | collective-permute-done | bytes 983072 | tf_op jit(solution)/shard_map/ppermute | solution.py:52
  28.7 1.6 %collective-permute-start.1 = (bf16[2,320,768]{2,1,0:T(8,128)(2,1)S(1)}, bf16[2,320,768]{2,1,0:T(8,128)(2,1)S(1)}, u32[]{:S(2)}, u32[]{:S(2)}) collective-permute-start(bf16[2,320,768]{2,1,0:T(8,128)(2,1)S(1)} %collective-permute-done), channel_id=1, source_target_pairs={{0,4},{4,8},{8,12},{12,0},{1,5},{5,9},{9,13},{13,1},{2,6},{6,10},{... | collective-permute-start | bytes 2949128 | tf_op jit(solution)/shard_map/ppermute | solution.py:52
  30.2 21.7 %collective-permute-done.1 = bf16[2,320,768]{2,1,0:T(8,128)(2,1)S(1)} collective-permute-done((bf16[2,320,768]{2,1,0:T(8,128)(2,1)S(1)}, bf16[2,320,768]{2,1,0:T(8,128)(2,1)S(1)}, u32[]{:S(2)}, u32[]{:S(2)}) %collective-permute-start.1) | collective-permute-done | bytes 983072 | tf_op jit(solution)/shard_map/ppermute | solution.py:52
  51.9 0.9 collective-permute-start.2
  52.9 1.6 %convolution_convert_fusion.1 = bf16[640,384]{1,0:T(8,128)(2,1)S(1)} fusion(bf16[640,384]{1,0:T(8,128)(2,1)} %bitcast.171, bf16[384,1152]{1,0:T(8,128)(2,1)} %param.10), kind=kOutput, calls=%fused_computation.46 | convolution fusion | flops 188989440 | bytes 1277952 | tf_op jit(solution)/shard_map/dot_general | solution.py:42
  54.5 21.1 %collective-permute-done.2 = bf16[2,320,768]{2,1,0:T(8,128)(2,1)} collective-permute-done((bf16[2,320,768]{2,1,0:T(8,128)(2,1)S(1)}, bf16[2,320,768]{2,1,0:T(8,128)(2,1)}, u32[]{:S(2)}, u32[]{:S(2)}) %collective-permute-start.2) | collective-permute-done | bytes 983072 | tf_op jit(solution)/shard_map/ppermute | solution.py:52
  75.6 1.3 constant_dynamic-update-slice_fusion.7
  77.1 1.3 constant_dynamic-update-slice_fusion.3
  78.6 1.2 fusion.106
  79.8 0.6 fusion.1
  80.5 1.6 %fusion.19 = bf16[2,320,384]{2,1,0:T(8,128)(2,1)S(1)} fusion(bf16[2,2560,768]{2,1,0:T(8,128)(2,1)S(1)} %constant_dynamic-update-slice_fusion, s32[]{:T(128)S(6)} %select_n.101, s32[]{:T(128)S(6)} %add.186, f32[2,320,1280]{2,1,0:T(8,128)S(1)} %get-tuple-element.53, f32[2,320]{1,0:T(2,128)S(1)} %broadcast_maximum_fusion, f32[2,320]{1,0:T(2,128)S(1)} %fusion.1), kind=kOutput, calls=%fused_computation.56 | convolution fusion | flops 631275520 | bytes 5740552 | tf_op jit(solution)/shard_map/fqk,fkc->fqc/dot_general | solution.py:66
  82.0 0.6 fusion.24
  83.1 1.9 %collective-permute-start.3 = (bf16[2,2,160,384]{3,2,1,0:T(8,128)(2,1)S(1)}, bf16[2,2,160,384]{3,2,1,0:T(8,128)(2,1)S(1)}, u32[]{:S(2)}, u32[]{:S(2)}) collective-permute-start(bf16[2,2,160,384]{3,2,1,0:T(8,128)(2,1)S(1)} %multiply_convert_fusion), channel_id=1, source_target_pairs={{0,1},{1,2},{2,3},{4,5},{5,6},{6,7},{8,9},{9,10},{10,11},{12,13},{... | collective-permute-start | bytes 1474568 | tf_op jit(solution)/shard_map/ppermute | solution.py:12
  85.0 8.2 %collective-permute-done.3 = bf16[2,2,160,384]{3,2,1,0:T(8,128)(2,1)S(1)} collective-permute-done((bf16[2,2,160,384]{3,2,1,0:T(8,128)(2,1)S(1)}, bf16[2,2,160,384]{3,2,1,0:T(8,128)(2,1)S(1)}, u32[]{:S(2)}, u32[]{:S(2)}) %collective-permute-start.3) | collective-permute-done | bytes 491552 | tf_op jit(solution)/shard_map/ppermute | solution.py:12
  93.2 0.9 fusion.36
  94.1 5.4 %collective-permute-start.5 = (bf16[4,1,160,384]{3,2,1,0:T(8,128)(2,1)}, bf16[4,1,160,384]{3,2,1,0:T(8,128)(2,1)S(1)}, u32[]{:S(2)}, u32[]{:S(2)}) collective-permute-start(bf16[4,1,160,384]{3,2,1,0:T(8,128)(2,1)} %get-tuple-element.35), channel_id=1, source_target_pairs={{4,0},{8,4},{12,8},{5,1},{9,5},{13,9},{6,2},{10,6},{14,10},{7,3},{... | collective-permute-start | bytes 1474568 | tf_op jit(solution)/shard_map/ppermute | solution.py:23
  99.6 1.9 %collective-permute-start.4 = (bf16[4,1,160,384]{3,2,1,0:T(8,128)(2,1)S(1)}, bf16[4,1,160,384]{3,2,1,0:T(8,128)(2,1)S(1)}, u32[]{:S(2)}, u32[]{:S(2)}) collective-permute-start(bf16[4,1,160,384]{3,2,1,0:T(8,128)(2,1)S(1)} %get-tuple-element.34), channel_id=1, source_target_pairs={{0,4},{4,8},{8,12},{1,5},{5,9},{9,13},{2,6},{6,10},{10,14},{3,7},{... | collective-permute-start | bytes 1474568 | tf_op jit(solution)/shard_map/ppermute | solution.py:22
  102.1 4.2 %collective-permute-done.5 = bf16[4,1,160,384]{3,2,1,0:T(8,128)(2,1)S(1)} collective-permute-done((bf16[4,1,160,384]{3,2,1,0:T(8,128)(2,1)}, bf16[4,1,160,384]{3,2,1,0:T(8,128)(2,1)S(1)}, u32[]{:S(2)}, u32[]{:S(2)}) %collective-permute-start.5) | collective-permute-done | bytes 491552 | tf_op jit(solution)/shard_map/ppermute | solution.py:23
  106.2 4.1 %collective-permute-done.4 = bf16[4,1,160,384]{3,2,1,0:T(8,128)(2,1)S(1)} collective-permute-done((bf16[4,1,160,384]{3,2,1,0:T(8,128)(2,1)S(1)}, bf16[4,1,160,384]{3,2,1,0:T(8,128)(2,1)S(1)}, u32[]{:S(2)}, u32[]{:S(2)}) %collective-permute-start.4) | collective-permute-done | bytes 491552 | tf_op jit(solution)/shard_map/ppermute | solution.py:22
  110.3 1.2 select_maximum_fusion
  111.5 1.4 %slice_select_fusion = (bf16[2,2,160,384]{3,2,1,0:T(8,128)(2,1)S(1)}, bf16[2,2,160,384]{3,2,1,0:T(8,128)(2,1)S(1)}, bf16[2,2,160,384]{3,2,1,0:T(8,128)(2,1)S(1)}...) fusion(bf16[4,4,162,384]{3,2,1,0:T(8,128)(2,1)S(1)} %select_max, ...), kind=kLoop, calls=%fused_computation.72 | loop fusion | flops 2949120 | bytes 11796484 | tf_op jit(solution)/shard_map/jit(_where)/select_n | solution.py:96
  113.2 1.5 %slice_select_fusion.6 = (bf16[2,2,160,384]{3,2,1,0:T(8,128)(2,1)S(1)}, bf16[2,2,160,384]{3,2,1,0:T(8,128)(2,1)S(1)}, bf16[2,2,160,384]{3,2,1,0:T(8,128)(2,1)S(1...) fusion(bf16[4,3,160,384]{3,2,1,0:T(8,128)(2,1)S(1)} %get-tuple-, ...), kind=kLoop, calls=%fused_computation.78 | loop fusion | flops 3686400 | bytes 13762566 | tf_op jit(solution)/shard_map/jit(_where)/select_n | solution.py:96
  115.0 1.3 %slice-done.1 = s8[4194304]{0:T(1024)(128)(4,1)S(1)} async-done(((s8[7962624]{0:T(1024)(128)(4,1)}), s8[4194304]{0:T(1024)(128)(4,1)S(1)}, s32[]{:S(2)}) %slice-start.1) | async-done | bytes 4194328
  117.2 0.5 convolution_add_fusion.24
  117.7 0.5 convolution_add_fusion.23
  118.2 0.5 convolution_add_fusion.22
  118.6 0.5 fusion.11
  119.1 0.5 convolution_add_fusion.20
  119.6 0.5 convolution_add_fusion.19
  120.0 0.5 convolution_add_fusion.18
  120.5 0.5 convolution_add_fusion.17
  121.0 0.5 convolution_add_fusion.16
  121.4 0.5 convolution_add_fusion.15
  121.9 0.5 convolution_add_fusion.14
  122.4 0.5 convolution_add_fusion.13
  122.8 0.5 convolution_add_fusion.12
  123.3 0.5 convolution_add_fusion.11
  124.2 0.5 convolution_add_fusion.9
  125.6 0.5 convolution_add_fusion.6
  126.0 0.5 convolution_add_fusion.5
  126.5 0.6 convolution_add_fusion.4
  127.2 0.5 convolution_add_fusion.3
  127.6 0.5 convolution_add_fusion.2
  128.6 1.2 fusion.13
  (42 shorter events, 4.6 us)
Async XLA Ops:
  0.6 81.4 %copy-start = (bf16[384,384]{1,0:T(8,128)(2,1)S(1)}, bf16[384,384]{1,0:T(8,128)(2,1)}, u32[]{:S(2)}) copy-start(bf16[384,384]{1,0:T(8,128)(2,1)} %param.11) | copy-start | bytes 884740
  3.2 48.7 %copy-start.3 = (bf16[2,2,160,384]{3,2,1,0:T(8,128)(2,1)}, bf16[2,2,160,384]{3,2,1,0:T(8,128)(2,1)S(1)}, u32[]{:S(2)}) copy-start(bf16[2,2,160,384]{3,2,1,0:T(8,128)(2,1)S(1)} %multiply_convert_fusion.1) | copy-start | bytes 1474564
  5.1 23.5 %collective-permute-start = (bf16[2,320,768]{2,1,0:T(8,128)(2,1)S(1)}, bf16[2,320,768]{2,1,0:T(8,128)(2,1)S(1)}, u32[]{:S(2)}, u32[]{:S(2)}) collective-permute-start(bf16[2,320,768]{2,1,0:T(8,128)(2,1)S(1)} %bitcast.150), channel_id=1, source_target_pairs={{0,4},{4,8},{8,12},{12,0},{1,5},{5,9},{9,13},{13,1},{2,6},{6,10},{... | collective-permute-start | bytes 2949128 | tf_op jit(solution)/shard_map/ppermute | solution.py:52
  28.7 23.3 %collective-permute-start.1 = (bf16[2,320,768]{2,1,0:T(8,128)(2,1)S(1)}, bf16[2,320,768]{2,1,0:T(8,128)(2,1)S(1)}, u32[]{:S(2)}, u32[]{:S(2)}) collective-permute-start(bf16[2,320,768]{2,1,0:T(8,128)(2,1)S(1)} %collective-permute-done), channel_id=1, source_target_pairs={{0,4},{4,8},{8,12},{12,0},{1,5},{5,9},{9,13},{13,1},{2,6},{6,10},{... | collective-permute-start | bytes 2949128 | tf_op jit(solution)/shard_map/ppermute | solution.py:52
  51.9 23.7 %collective-permute-start.2 = (bf16[2,320,768]{2,1,0:T(8,128)(2,1)S(1)}, bf16[2,320,768]{2,1,0:T(8,128)(2,1)}, u32[]{:S(2)}, u32[]{:S(2)}) collective-permute-start(bf16[2,320,768]{2,1,0:T(8,128)(2,1)S(1)} %collective-permute-done.1), channel_id=1, source_target_pairs={{0,4},{4,8},{8,12},{12,0},{1,5},{5,9},{9,13},{13,1},{2,6},{6,10},{... | collective-permute-start | bytes 2949128 | tf_op jit(solution)/shard_map/ppermute | solution.py:52
  78.6 3.4 %copy-start.2 = (bf16[2,2,160,384]{3,2,1,0:T(8,128)(2,1)S(1)}, bf16[2,2,160,384]{3,2,1,0:T(8,128)(2,1)}, u32[]{:S(2)}) copy-start(bf16[2,2,160,384]{3,2,1,0:T(8,128)(2,1)} %param.7) | copy-start | bytes 1474564
  79.8 2.9 %copy-start.5 = (f32[384]{0:T(512)S(1)}, f32[384]{0:T(512)}, u32[]{:S(2)}) copy-start(f32[384]{0:T(512)} %param.12) | copy-start | bytes 4612
  79.8 21.7 %copy-start.6 = (s32[4]{0:T(128)S(1)}, s32[4]{0:T(128)}, u32[]{:S(2)}) copy-start(s32[4]{0:T(128)} %param.8) | copy-start | bytes 52
  82.6 43.9 %copy-start.4 = (bf16[640,384]{1,0:T(8,128)(2,1)}, bf16[640,384]{1,0:T(8,128)(2,1)S(1)}, u32[]{:S(2)}) copy-start(bf16[640,384]{1,0:T(8,128)(2,1)S(1)} %get-tuple-element.55) | copy-start | bytes 1474564
  83.1 10.1 %collective-permute-start.3 = (bf16[2,2,160,384]{3,2,1,0:T(8,128)(2,1)S(1)}, bf16[2,2,160,384]{3,2,1,0:T(8,128)(2,1)S(1)}, u32[]{:S(2)}, u32[]{:S(2)}) collective-permute-start(bf16[2,2,160,384]{3,2,1,0:T(8,128)(2,1)S(1)} %multiply_convert_fusion), channel_id=1, source_target_pairs={{0,1},{1,2},{2,3},{4,5},{5,6},{6,7},{8,9},{9,10},{10,11},{12,13},{... | collective-permute-start | bytes 1474568 | tf_op jit(solution)/shard_map/ppermute | solution.py:12
  94.1 12.1 %collective-permute-start.5 = (bf16[4,1,160,384]{3,2,1,0:T(8,128)(2,1)}, bf16[4,1,160,384]{3,2,1,0:T(8,128)(2,1)S(1)}, u32[]{:S(2)}, u32[]{:S(2)}) collective-permute-start(bf16[4,1,160,384]{3,2,1,0:T(8,128)(2,1)} %get-tuple-element.35), channel_id=1, source_target_pairs={{4,0},{8,4},{12,8},{5,1},{9,5},{13,9},{6,2},{10,6},{14,10},{7,3},{... | collective-permute-start | bytes 1474568 | tf_op jit(solution)/shard_map/ppermute | solution.py:23
  99.6 10.7 %collective-permute-start.4 = (bf16[4,1,160,384]{3,2,1,0:T(8,128)(2,1)S(1)}, bf16[4,1,160,384]{3,2,1,0:T(8,128)(2,1)S(1)}, u32[]{:S(2)}, u32[]{:S(2)}) collective-permute-start(bf16[4,1,160,384]{3,2,1,0:T(8,128)(2,1)S(1)} %get-tuple-element.34), channel_id=1, source_target_pairs={{0,4},{4,8},{8,12},{1,5},{5,9},{9,13},{2,6},{6,10},{10,14},{3,7},{... | collective-permute-start | bytes 1474568 | tf_op jit(solution)/shard_map/ppermute | solution.py:22
  112.9 2.1 %slice-start = ((s8[7962624]{0:T(1024)(128)(4,1)}), s8[3768320]{0:T(1024)(128)(4,1)S(1)}, s32[]{:S(2)}) async-start(s8[7962624]{0:T(1024)(128)(4,1)} %bitcast.148), calls=%async_computation | async-start | bytes 7536640
  113.2 3.1 %slice-start.1 = ((s8[7962624]{0:T(1024)(128)(4,1)}), s8[4194304]{0:T(1024)(128)(4,1)S(1)}, s32[]{:S(2)}) async-start(s8[7962624]{0:T(1024)(128)(4,1)} %bitcast.148), calls=%async_computation.1 | async-start | bytes 8388608
  126.0 3.8 %copy-start.1 = (bf16[384,384]{1,0:T(8,128)(2,1)S(1)}, bf16[384,384]{1,0:T(8,128)(2,1)}, u32[]{:S(2)}) copy-start(bf16[384,384]{1,0:T(8,128)(2,1)} %param.11) | copy-start | bytes 884740
